TPU v7x, 32 devices: a whole 2x2x4 slice. The times are simulated.
32 devices in a mesh: grp: 2 (over y), patch: 4 (over z), lead: 4 (over x, core).
Axes of the slice: x: 2, y: 2, z: 4, core: 2. Of those that a mesh axis runs over, the one named last changes fastest.
Arguments:
- features: bfloat16 [8, 4, 128, 32, 128], P(('grp', 'lead'), 'patch'), parts along dimension 0, may hold values from -6 to 6
- context: bfloat16 [4, 8, 128, 2048], P('patch', ('grp', 'lead')), parts along dimension 1, may hold values from -6 to 6
- owner: int32 [8], P('grp'), parts along dimension 0, may hold values from 0 to 3, as said below
- hours: int32 [8], P('grp'), parts along dimension 0, may hold values from 0 to 18, as said below
- w_first: bfloat16 [9, 192, 128], replicated, may hold values from -0.15625 to 0.15625
- w_second: bfloat16 [9, 128, 128], replicated, may hold values from -0.1875 to 0.1875
- w_lead_in: bfloat16 [128, 32], replicated, may hold values from -0.5 to 0.5
- w_lead_mix: bfloat16 [3, 32, 32], replicated, may hold values from -0.625 to 0.625
- w_lead_out: bfloat16 [32, 128], replicated, may hold values from -1 to 1
Outputs:
- updated: bfloat16 [8, 4, 128, 32, 128], P(('grp', 'lead'), 'patch'), parts along dimension 0
There are 2 independent parts, one for each index of `grp`. A program takes and returns all parts, laid end to end along the dimension named above; an argument that names none is the same for every part. Nothing has to cross between parts.
Inputs may be any that keep to these rules, and one draw needn't show every extreme that they name: `owner`: values are patch indices; some lead hour is owned by patch 0 and some by patch 4 - 1. `hours`: strictly increasing along the lead hours; consecutive differences run from 1 to 6, both reached; the last lead hour is the largest value.
All inputs are finite; a program needn't handle non-finite values.
Results may differ from a plain program's by a relative error of at most 0.0037.
Values may be sent and summed in bfloat16 or wider, within the bound.
A program may use at most 64 MiB of HBM per device.

v0:
```python
import functools

import jax
import jax.numpy as jnp
from jax import lax
from jax.experimental import pallas as pl
from jax.experimental.pallas import tpu as pltpu
from jax.sharding import PartitionSpec as P

MESH = pl.DeviceIdType.MESH
ROWS = 16
SLICE = 8
LAG = 4
F32 = jnp.float32
BF16 = jnp.bfloat16


def silu(v):
    return 0.5 * v * (1.0 + jnp.tanh(0.5 * v))


def dot(a, b):
    return jnp.dot(a, b, preferred_element_type=F32)


def kernel(
    n, leads, owner_ref, hours_ref, f_hbm, c_hbm, w1_hbm, w2_hbm, wi_hbm, wm_hbm, wo_hbm, o_ref,
    f_ref, c_ref, w1_ref, w2_ref, wi_ref, wm_ref, wo_ref,
    xs, ys, acc, big_g, gt, ct, wf, wc, ws, wd, wp, wx, proj, prev, foll, mixed,
    up_in, down_in, up_out, down_out, in_sem,
    up_send, up_recv, down_send, down_recv, lead_send, lead_recv,
):
    height, width, ch = f_ref.shape
    chunks = height // ROWS
    slices = height // SLICE
    half = ROWS // 2
    cells = ROWS * width
    ctx_ch = c_ref.shape[2] // width
    per = ch // ctx_ch
    groups = width // per
    temporal = wi_ref.shape[0]
    packs = ch // temporal
    packed_rows = height * width // packs

    def fetch(i):
        source, target = (
            (f_hbm, f_ref), (wi_hbm, wi_ref), (c_hbm, c_ref), (w1_hbm, w1_ref), (w2_hbm, w2_ref),
            (wm_hbm, wm_ref), (wo_hbm, wo_ref),
        )[i]
        return pltpu.make_async_copy(source, target, in_sem.at[i])

    z = lax.axis_index("patch")
    lead = lax.axis_index("lead")
    owner = owner_ref[lead]
    first, last = z == 0, z == n - 1
    lead_first, lead_last = lead == 0, lead == leads - 1

    barrier = pltpu.get_barrier_semaphore()


    for cond, axis, index in (
        (jnp.logical_not(first), "patch", z - 1),
        (jnp.logical_not(last), "patch", z + 1),
        (jnp.logical_not(lead_first), "lead", lead - 1),
        (jnp.logical_not(lead_last), "lead", lead + 1),
    ):
        @pl.when(cond)
        def _(axis=axis, index=index):
            pl.semaphore_signal(barrier, inc=1, device_id={axis: index}, device_id_type=MESH)

    neighbours = (
        4
        - first.astype(jnp.int32)
        - last.astype(jnp.int32)
        - lead_first.astype(jnp.int32)
        - lead_last.astype(jnp.int32)
    )
    for i in range(7):
        fetch(i).start()

    pl.semaphore_wait(barrier, neighbours)

    def up_copy(src, c):
        return pltpu.make_async_remote_copy(
            src_ref=src.at[c], dst_ref=up_in.at[c], send_sem=up_send.at[c],
            recv_sem=up_recv.at[c], device_id={"patch": z + 1}, device_id_type=MESH,
        )

    def down_copy(src, c):
        return pltpu.make_async_remote_copy(
            src_ref=src.at[c], dst_ref=down_in.at[c], send_sem=down_send.at[c],
            recv_sem=down_recv.at[c], device_id={"patch": z - 1}, device_id_type=MESH,
        )

    @pl.when(first)
    def _():
        @pl.loop(0, slices)
        def _(c):
            up_copy(c_hbm, c).start()

    @pl.when(last)
    def _():
        @pl.loop(0, slices)
        def _(c):
            down_copy(c_hbm, c).start()

    def project():
        fetch(0).wait()
        fetch(1).wait()
        wp[...] = jnp.zeros_like(wp)
        parts = []
        rows_q = height // packs
        for q in range(packs):
            wp[q * temporal : (q + 1) * temporal, q * ch : (q + 1) * ch] = wi_ref[...]
            parts.append(f_ref[q * rows_q : (q + 1) * rows_q].reshape(packed_rows, ch))
        total = lax.dot_general(
            jnp.concatenate(parts, axis=1), wp[...], (((1,), (1,)), ((), ())),
            preferred_element_type=F32,
        )
        proj[...] = total.astype(BF16)

    def pack_weights(target, source):
        zero = jnp.zeros((ch, ch), BF16)
        for r in range(4):
            for b in range(3):
                at = (3 * r + b) * ch
                for q in range(2):
                    a = r - q
                    block = source[3 * a + b, :ch, :] if 0 <= a <= 2 else zero
                    target[at : at + ch, q * ch : (q + 1) * ch] = block

    def pack_context_weights():
        small = jnp.zeros((ctx_ch, ch), BF16)
        for a in range(3):
            taps = [w1_ref[3 * a + b, ch:, :] for b in range(3)]
            for i, pair in enumerate(
                ((taps[1], taps[0]), (taps[2], taps[1]), (taps[0], small), (small, taps[2]))
            ):
                at = a * 4 * ctx_ch + i * ctx_ch
                for q in range(2):
                    wc[at : at + ctx_ch, q * ch : (q + 1) * ch] = pair[q]

    def pack_lead_weights():
        wd[...] = jnp.zeros_like(wd)
        wx[...] = jnp.zeros_like(wx)
        for q in range(packs):
            at = slice(q * temporal, (q + 1) * temporal)
            for t in range(3):
                wd[t, at, at] = wm_ref[t]
            wx[q, at, :] = wo_ref[...]

    col = lax.rem(lax.broadcasted_iota(jnp.int32, (cells, ch), 0), width)

    def put_shifted(target, v, k):
        left = jnp.where(col == 0, 0.0, pltpu.roll(v, 1, 0))
        right = jnp.where(col == width - 1, 0.0, pltpu.roll(v, cells - 1, 0))
        for b, value in enumerate((left, v, right)):
            target[b, pl.ds(1 + k * ROWS, ROWS)] = value.astype(BF16).reshape(ROWS, width, ch)

    def clear_edges():
        edge = jnp.zeros((width, ch), BF16)
        for target in (xs, ys):
            for b in range(3):
                target[b, 0] = edge
                target[b, height + 1] = edge
        big_g[0] = jnp.zeros(big_g.shape[1:], BF16)
        big_g[height + 1] = jnp.zeros(big_g.shape[1:], BF16)

    def shift_features():
        @pl.loop(0, chunks)
        def _(k):
            put_shifted(xs, f_ref[pl.ds(k * ROWS, ROWS)].reshape(cells, ch).astype(F32), k)

    def lead_copy(side):
        landing, index = ((prev, lead + 1), (foll, lead - 1))[side]
        return pltpu.make_async_remote_copy(
            src_ref=proj, dst_ref=landing, send_sem=lead_send.at[side],
            recv_sem=lead_recv.at[side], device_id={"lead": index}, device_id_type=MESH,
        )

    def send_projection():
        @pl.when(jnp.logical_not(lead_last))
        def _():
            lead_copy(0).start()

        @pl.when(jnp.logical_not(lead_first))
        def _():
            lead_copy(1).start()

    def conv_pairs(source, weights, k, count=1):
        pairs = count * half
        parts = [
            source[b, pl.ds(k * ROWS, count * ROWS + 2)].reshape(pairs + 1, 2, width, ch)
            for b in range(3)
        ]
        lhs = [
            parts[b][r // 2 : r // 2 + pairs, r % 2].reshape(pairs * width, ch)
            for r in range(4)
            for b in range(3)
        ]
        return dot(jnp.concatenate(lhs, axis=1), weights[...])

    def feature_conv(k):
        out = conv_pairs(xs, wf, k)
        for q in range(2):
            acc[k, :, q] = out[:, q * ch : (q + 1) * ch].reshape(half, width, ch)

    def mix():
        @pl.when(jnp.logical_not(lead_first))
        def _():
            lead_copy(0).wait_recv()

        @pl.when(jnp.logical_not(lead_last))
        def _():
            lead_copy(1).wait_recv()

        @pl.when(lead_first)
        def _():
            prev[...] = jnp.zeros_like(prev)

        @pl.when(lead_last)
        def _():
            foll[...] = jnp.zeros_like(foll)

        now = hours_ref[lead]
        before = hours_ref[jnp.maximum(lead - 1, 0)]
        after = hours_ref[jnp.minimum(lead + 1, leads - 1)]

        def gain(later, earlier, absent):
            gap = jnp.full((1, ch), (later - earlier).astype(F32), F32)
            return jnp.where(absent, 0.0, jnp.exp(-0.5 * (gap - 1.0)))

        gain_prev = gain(now, before, lead_first)
        gain_next = gain(after, now, lead_last)
        value = gain_prev * dot(prev[...], wd[0])
        value = value + dot(proj[...], wd[1])
        value = value + gain_next * dot(foll[...], wd[2])
        mixed[...] = value.astype(BF16)

    total_rows = SLICE * groups
    lane = lax.broadcasted_iota(jnp.int32, (total_rows, ch), 1)
    group = lax.rem(lax.broadcasted_iota(jnp.int32, (total_rows, ch), 0), groups)

    def take_context(k):
        low = jnp.where(owner < z, up_in[k], down_in[k])
        g = jnp.where(owner == z, c_ref[k], low).astype(F32)
        for j in range(groups):
            gt[pl.ds(j, SLICE, stride=groups), :] = g[:, j * ch : (j + 1) * ch]
        x = gt[...]
        y = pltpu.roll(x, ctx_ch, 1)
        back = jnp.where(group == 0, 0.0, pltpu.roll(y, 1, 0))
        ahead = jnp.where(group == groups - 1, 0.0, pltpu.roll(y, total_rows - 1, 0))
        beside = jnp.where(lane < ctx_ch, back, ahead)
        rows = pl.ds(1 + k * SLICE, SLICE)
        big_g[rows, :, :ch] = x.astype(BF16).reshape(SLICE, groups, ch)
        big_g[rows, :, ch:] = beside.astype(BF16).reshape(SLICE, groups, ch)

    def activate(k):
        lhs = [
            big_g[pl.ds(k * ROWS + a, ROWS)].reshape(ROWS * groups, 2 * ch) for a in range(3)
        ]
        out = dot(jnp.concatenate(lhs, axis=1), wc[...])
        for q in range(2):
            ct[pl.ds(q, ROWS * groups, stride=2), :] = out[:, q * ch : (q + 1) * ch]
        v = silu(ct[...] + acc[k].reshape(cells, ch))
        put_shifted(ys, v, k)

    per_pack = packed_rows // cells

    def finish(k, count=1):
        pairs, rows = count * half, pl.ds(k * ROWS, count * ROWS)
        out = conv_pairs(ys, ws, k, count)
        at = pl.multiple_of(lax.rem(k, per_pack) * cells, cells)
        lifted = dot(mixed[pl.ds(at, count * cells)], wx[k // per_pack])
        lifted = lifted.reshape(pairs, 2, width, ch)
        own = f_ref[rows].reshape(pairs, 2, width, ch)
        results = []
        for q in range(2):
            pre = out[:, q * ch : (q + 1) * ch].reshape(pairs, width, ch) + lifted[:, q]
            results.append((own[:, q].astype(F32) + silu(pre)).astype(BF16))
        o_ref[rows] = jnp.stack(results, axis=1).reshape(count * ROWS, width, ch)

    project()
    fetch(2).wait()
    up_at, down_at = LAG * z, LAG * (n - 1 - z)
    ready_at = jnp.maximum(up_at, down_at)

    @pl.loop(0, slices + 2 + LAG * (n - 1))
    def _(s):
        cu = s - up_at
        cd = s - down_at

        def go_up(here):
            @pl.when(here & (cu >= 0) & (cu < slices) & jnp.logical_not(first))
            def _():
                up_copy(c_ref, cu).wait_recv()

                @pl.when(jnp.logical_not(last))
                def _():
                    up_out[cu] = jnp.where(owner == z, c_ref[cu], up_in[cu])
                    up_copy(up_out, cu).start()

        up_first = up_at >= down_at
        go_up(up_first)

        @pl.when((cd >= 0) & (cd < slices) & jnp.logical_not(last))
        def _():
            down_copy(c_ref, cd).wait_recv()

            @pl.when(jnp.logical_not(first))
            def _():
                down_out[cd] = jnp.where(owner == z, c_ref[cd], down_in[cd])
                down_copy(down_out, cd).start()

        go_up(jnp.logical_not(up_first))

        @pl.when((s >= 2) & (s < chunks + 2))
        def _():
            feature_conv(s - 2)

        @pl.when(s == 0)
        def _():
            shift_features()
            send_projection()
            clear_edges()

        @pl.when(s == 1)
        def _():
            fetch(3).wait()
            pack_weights(wf, w1_ref)
            pack_context_weights()

        @pl.when(s == 3)
        def _():
            for i in (4, 5, 6):
                fetch(i).wait()
            pack_weights(ws, w2_ref)
            pack_lead_weights()

        @pl.when(s == 7)
        def _():
            mix()

        k = s - ready_at

        @pl.when((k >= 0) & (k < slices))
        def _():
            take_context(k)

        @pl.when((k >= 2) & (k <= slices) & (lax.rem(k, 2) == 0))
        def _():
            activate(lax.div(k, 2) - 1)

        @pl.when((k >= 5) & (k <= slices - 1) & (lax.rem(k, 2) == 1))
        def _():
            finish(lax.div(k - 5, 2))

        @pl.when(k == slices + 1)
        def _():
            finish(chunks - 2, 2)

    @pl.loop(0, slices)
    def _(c):
        @pl.when(jnp.logical_not(last))
        def _():
            up_copy(c_ref, c).wait_send()

        @pl.when(jnp.logical_not(first))
        def _():
            down_copy(c_ref, c).wait_send()

    @pl.when(jnp.logical_not(lead_last))
    def _():
        lead_copy(0).wait_send()

    @pl.when(jnp.logical_not(lead_first))
    def _():
        lead_copy(1).wait_send()


def per_device(
    features, context, owner, hours, w_first, w_second, w_lead_in, w_lead_mix, w_lead_out
):
    n, leads = lax.axis_size("patch"), lax.axis_size("lead")
    _, _, height, width, ch = features.shape
    temporal = w_lead_in.shape[1]
    merged = context.shape[3]
    chunks = height // ROWS
    cells = ROWS * width
    groups = merged // ch
    packs = ch // temporal
    packed_rows = height * width // packs
    vmem, smem = pltpu.VMEM, pl.BlockSpec(memory_space=pltpu.SMEM)
    slices = height // SLICE
    line = vmem((slices, SLICE, merged), BF16)
    hbm = pl.BlockSpec(memory_space=pl.ANY)
    dma = pltpu.SemaphoreType.DMA
    out = pl.pallas_call(
        functools.partial(kernel, n, leads),
        out_shape=vmem((height, width, ch), BF16),
        in_specs=[smem, smem] + [hbm] * 7,
        out_specs=pl.BlockSpec(memory_space=pltpu.VMEM),
        scratch_shapes=[
            vmem((height, width, ch), BF16),
            line,
            vmem(w_first.shape, BF16),
            vmem(w_second.shape, BF16),
            vmem((temporal, ch), BF16),
            vmem(w_lead_mix.shape, BF16),
            vmem(w_lead_out.shape, BF16),
            vmem((3, height + 2, width, ch), BF16),
            vmem((3, height + 2, width, ch), BF16),
            vmem((chunks, ROWS // 2, 2, width, ch), F32),
            vmem((height + 2, groups, 2 * ch), BF16),
            vmem((SLICE * groups, ch), F32),
            vmem((cells, ch), F32),
            vmem((12 * ch, 2 * ch), BF16),
            vmem((6 * ch, 2 * ch), BF16),
            vmem((12 * ch, 2 * ch), BF16),
            vmem((3, ch, ch), BF16),
            vmem((ch, packs * ch), BF16),
            vmem((packs, ch, ch), BF16),
            vmem((packed_rows, ch), BF16),
            vmem((packed_rows, ch), BF16),
            vmem((packed_rows, ch), BF16),
            vmem((packed_rows, ch), BF16),
            line, line, line, line,
            dma((7,)),
            dma((slices,)), dma((slices,)), dma((slices,)), dma((slices,)), dma((2,)), dma((2,)),
        ],
        compiler_params=pltpu.CompilerParams(collective_id=0, has_side_effects=True),
    )(
        owner, hours, features[0, 0], context.reshape(slices, SLICE, merged),
        w_first, w_second, w_lead_in.T, w_lead_mix, w_lead_out,
    )
    return out[None, None]


def solution(mesh):
    placed = (
        P(("grp", "lead"), "patch", None, None, None),
        P("patch", ("grp", "lead"), None, None),
        P("grp"),
        P("grp"),
        P(),
        P(),
        P(),
        P(),
        P(),
    )
    return jax.shard_map(
        per_device,
        mesh=mesh,
        in_specs=placed,
        out_specs=P(("grp", "lead"), "patch", None, None, None),
        check_vma=False,
    )
```

profile of v0, /device:TPU:0, one launch (start us, length us, event | category | flops | bytes accessed | tf_op | source)
XLA Modules:
  0.0 28.6 jit_solution(9862829281871169811)
XLA Ops:
  0.0 27.6 %shard_map.91 = bf16[128,32,128]{2,1,0:T(8,128)(2,1)S(1)} custom-call(s32[4]{0:T(128)} %owner_ref.1, s32[4]{0:T(128)} %hours_ref.1, bf16[128,32,128]{2,1,0:T(8,128)(2,1)} %bitcast.5, bf16[16,8,2048]{2,1,0:T(8,128)(2,1)} %bitcast.6, bf16[9,192,128]{2,1,0:T(8,128)(2,1)} %w1_hbm.1, bf16[9,128,128]{2,1,0:T(8,128)(2,1)} %w2_hbm.1, bf16[32,128]{1,0:T(8,128)(2,1)} %bitcast.7, ...), custom_call_target="tpu_custom_call" | custom-call | tf_op jit(solution)/shard_map/pallas_call | solution.py:398
  27.6 1.0 %copy.11 = bf16[1,1,128,32,128]{4,3,2,1,0:T(8,128)(2,1)} copy(bf16[1,1,128,32,128]{4,3,2,1,0:T(8,128)(2,1)S(1)} %bitcast.4) | data formatting | bytes 2097152
where the time goes:
time: 28.7 us; the launch traced here: 28.6 us
  Pallas kernels  27.6 us (96%)
  local copies, waits for them, and re-layouts  0.97 us (3%)
    pallas_call x1, Pallas kernels, per_device(): pl.pallas_call(functools.partial(kernel, n, leads), out_shape=vmem((heigh...  27.6 us
    unnamed x1, local copies, waits for them, and re-layouts  0.97 us

commit v1 on v0

v1 whole, which is shorter than its diff:
```python
import functools

import jax
import jax.numpy as jnp
from jax import lax
from jax.experimental import pallas as pl
from jax.experimental.pallas import tpu as pltpu
from jax.sharding import PartitionSpec as P

MESH = pl.DeviceIdType.MESH
ROWS = 16
SLICE = 8
HALVES = 2
LAG = 9
ACT = 3
FIN = 5
F32 = jnp.float32
BF16 = jnp.bfloat16


def silu(v):
    return 0.5 * v * (1.0 + jnp.tanh(0.5 * v))


def dot(a, b):
    return jnp.dot(a, b, preferred_element_type=F32)


def kernel(
    n, leads, owner_hbm, hours_hbm, f_hbm, c_hbm, w1_hbm, w2_hbm, wi_hbm, wm_hbm, wo_hbm, o_ref,
    f_ref, c_ref, w1_ref, w2_ref, wi_ref, wm_ref, wo_ref,
    xs, ys, acc, big_g, gt, ct, wf, wc, ws, wd, wp, wx, proj, prev, foll, mixed,
    up_in, down_in, up_out, down_out, owner_ref, hours_ref, small_sem, in_sem,
    up_send, up_recv, down_send, down_recv, lead_send, lead_recv,
):
    height, width, ch = f_ref.shape
    chunks = height // ROWS
    slices = height // SLICE
    half = ROWS // 2
    cells = ROWS * width
    part = c_ref.shape[3]
    ctx_ch = HALVES * part // width
    pieces = HALVES * slices
    per = ch // ctx_ch
    groups = width // per
    temporal = wi_ref.shape[0]
    packs = ch // temporal
    packed_rows = height * width // packs

    def fetch(i):
        source, target = (
            (f_hbm, f_ref), (wi_hbm, wi_ref), (w1_hbm, w1_ref), (w2_hbm, w2_ref),
            (wm_hbm, wm_ref), (wo_hbm, wo_ref), (owner_hbm, owner_ref), (hours_hbm, hours_ref),
        )[i]
        return pltpu.make_async_copy(source, target, in_sem.at[i])

    def fetch_context(half):
        return pltpu.make_async_copy(
            c_hbm.at[:, :, half * part : (half + 1) * part], c_ref.at[:, half], small_sem.at[half]
        )

    z = lax.axis_index("patch")
    lead = lax.axis_index("lead")
    first, last = z == 0, z == n - 1
    lead_first, lead_last = lead == 0, lead == leads - 1

    barrier = pltpu.get_barrier_semaphore()


    for cond, axis, index in (
        (jnp.logical_not(first), "patch", z - 1),
        (jnp.logical_not(last), "patch", z + 1),
        (jnp.logical_not(lead_first), "lead", lead - 1),
        (jnp.logical_not(lead_last), "lead", lead + 1),
    ):
        @pl.when(cond)
        def _(axis=axis, index=index):
            pl.semaphore_signal(barrier, inc=1, device_id={axis: index}, device_id_type=MESH)

    neighbours = (
        4
        - first.astype(jnp.int32)
        - last.astype(jnp.int32)
        - lead_first.astype(jnp.int32)
        - lead_last.astype(jnp.int32)
    )
    for i in (6, 7, 0, 1):
        fetch(i).start()
    for half in range(HALVES):
        fetch_context(half).start()
    for i in range(2, 6):
        fetch(i).start()

    pl.semaphore_wait(barrier, neighbours)

    def up_copy(src, c, half):
        at = HALVES * c + half
        return pltpu.make_async_remote_copy(
            src_ref=src, dst_ref=up_in.at[c, half], send_sem=up_send.at[at],
            recv_sem=up_recv.at[at], device_id={"patch": z + 1}, device_id_type=MESH,
        )

    def down_copy(src, c, half):
        at = HALVES * c + half
        return pltpu.make_async_remote_copy(
            src_ref=src, dst_ref=down_in.at[c, half], send_sem=down_send.at[at],
            recv_sem=down_recv.at[at], device_id={"patch": z - 1}, device_id_type=MESH,
        )

    @pl.when(first)
    def _():
        @pl.loop(0, slices)
        def _(c):
            for half in range(HALVES):
                up_copy(c_hbm.at[c, :, half * part : (half + 1) * part], c, half).start()

    @pl.when(last)
    def _():
        @pl.loop(0, slices)
        def _(c):
            for half in range(HALVES):
                down_copy(c_hbm.at[c, :, half * part : (half + 1) * part], c, half).start()

    def project():
        fetch(0).wait()
        fetch(1).wait()
        wp[...] = jnp.zeros_like(wp)
        parts = []
        whole = f_ref[...].reshape(height // packs, packs, width, ch)
        for q in range(packs):
            wp[q * temporal : (q + 1) * temporal, q * ch : (q + 1) * ch] = wi_ref[...]
            parts.append(whole[:, q].reshape(packed_rows, ch))
        total = lax.dot_general(
            jnp.concatenate(parts, axis=1), wp[...], (((1,), (1,)), ((), ())),
            preferred_element_type=F32,
        )
        proj[...] = total.astype(BF16)

    def pack_weights(target, source):
        zero = jnp.zeros((ch, ch), BF16)
        for r in range(4):
            for b in range(3):
                at = (3 * r + b) * ch
                for q in range(2):
                    a = r - q
                    block = source[3 * a + b, :ch, :] if 0 <= a <= 2 else zero
                    target[at : at + ch, q * ch : (q + 1) * ch] = block

    def pack_context_weights():
        small = jnp.zeros((ctx_ch, ch), BF16)
        for a in range(3):
            taps = [w1_ref[3 * a + b, ch:, :] for b in range(3)]
            for i, pair in enumerate(
                ((taps[1], taps[0]), (taps[2], taps[1]), (taps[0], small), (small, taps[2]))
            ):
                at = a * 4 * ctx_ch + i * ctx_ch
                for q in range(2):
                    wc[at : at + ctx_ch, q * ch : (q + 1) * ch] = pair[q]

    def pack_lead_weights():
        wd[...] = jnp.zeros_like(wd)
        wx[...] = jnp.zeros_like(wx)
        for q in range(packs):
            at = slice(q * temporal, (q + 1) * temporal)
            for t in range(3):
                wd[t, at, at] = wm_ref[t]
            wx[at, q * ch : (q + 1) * ch] = wo_ref[...]

    def put_shifted(target, v, row, count):
        size = count * width
        col = lax.rem(lax.broadcasted_iota(jnp.int32, (size, ch), 0), width)
        left = jnp.where(col == 0, 0.0, pltpu.roll(v, 1, 0))
        right = jnp.where(col == width - 1, 0.0, pltpu.roll(v, size - 1, 0))
        for b, value in enumerate((left, v, right)):
            target[b, pl.ds(1 + row, count)] = value.astype(BF16).reshape(count, width, ch)

    def clear_edges():
        edge = jnp.zeros((width, ch), BF16)
        for target in (xs, ys):
            for b in range(3):
                target[b, 0] = edge
                target[b, height + 1] = edge
        big_g[0] = jnp.zeros(big_g.shape[1:], BF16)
        big_g[height + 1] = jnp.zeros(big_g.shape[1:], BF16)

    def shift_features():
        @pl.loop(0, chunks)
        def _(k):
            put_shifted(xs, f_ref[pl.ds(k * ROWS, ROWS)].reshape(cells, ch).astype(F32), k * ROWS, ROWS)

    def lead_copy(side):
        landing, index = ((prev, lead + 1), (foll, lead - 1))[side]
        return pltpu.make_async_remote_copy(
            src_ref=proj, dst_ref=landing, send_sem=lead_send.at[side],
            recv_sem=lead_recv.at[side], device_id={"lead": index}, device_id_type=MESH,
        )

    def send_projection():
        @pl.when(jnp.logical_not(lead_last))
        def _():
            lead_copy(0).start()

        @pl.when(jnp.logical_not(lead_first))
        def _():
            lead_copy(1).start()

    def conv_pairs(source, weights, row, count):
        pairs = count // 2
        parts = [
            source[b, pl.ds(row, count + 2)].reshape(pairs + 1, 2, width, ch) for b in range(3)
        ]
        lhs = [
            parts[b][r // 2 : r // 2 + pairs, r % 2].reshape(pairs * width, ch)
            for r in range(4)
            for b in range(3)
        ]
        return dot(jnp.concatenate(lhs, axis=1), weights[...])

    def split_pairs(out, count):
        return [
            out[:, q * ch : (q + 1) * ch].reshape(count // 2, width, ch) for q in range(2)
        ]

    def feature_conv(k):
        out = split_pairs(conv_pairs(xs, wf, k * ROWS, ROWS), ROWS)
        acc[pl.ds(k * ROWS, ROWS)] = jnp.stack(out, axis=1).reshape(ROWS, width, ch)

    def mix():
        @pl.when(jnp.logical_not(lead_first))
        def _():
            lead_copy(0).wait_recv()

        @pl.when(jnp.logical_not(lead_last))
        def _():
            lead_copy(1).wait_recv()

        @pl.when(lead_first)
        def _():
            prev[...] = jnp.zeros_like(prev)

        @pl.when(lead_last)
        def _():
            foll[...] = jnp.zeros_like(foll)

        now = hours_ref[lead]
        before = hours_ref[jnp.maximum(lead - 1, 0)]
        after = hours_ref[jnp.minimum(lead + 1, leads - 1)]

        def gain(later, earlier, absent):
            gap = jnp.full((1, ch), (later - earlier).astype(F32), F32)
            return jnp.where(absent, 0.0, jnp.exp(-0.5 * (gap - 1.0)))

        gain_prev = gain(now, before, lead_first)
        gain_next = gain(after, now, lead_last)
        value = gain_prev * dot(prev[...], wd[0])
        value = value + dot(proj[...], wd[1])
        value = value + gain_next * dot(foll[...], wd[2])
        mixed[...] = value.astype(BF16)

    total_rows = SLICE * groups

    def take_context(k):
        lane = lax.broadcasted_iota(jnp.int32, (total_rows, ch), 1)
        group = lax.rem(lax.broadcasted_iota(jnp.int32, (total_rows, ch), 0), groups)
        owner = owner_ref[lead]
        per_half = groups // HALVES
        for half in range(HALVES):
            low = jnp.where(owner < z, up_in[k, half], down_in[k, half])
            g = jnp.where(owner == z, c_ref[k, half], low).astype(F32)
            for j in range(per_half):
                at = half * per_half + j
                gt[pl.ds(at, SLICE, stride=groups), :] = g[:, j * ch : (j + 1) * ch]
        x = gt[...]
        y = pltpu.roll(x, ctx_ch, 1)
        back = jnp.where(group == 0, 0.0, pltpu.roll(y, 1, 0))
        ahead = jnp.where(group == groups - 1, 0.0, pltpu.roll(y, total_rows - 1, 0))
        beside = jnp.where(lane < ctx_ch, back, ahead)
        rows = pl.ds(1 + k * SLICE, SLICE)
        big_g[rows, :, :ch] = x.astype(BF16).reshape(SLICE, groups, ch)
        big_g[rows, :, ch:] = beside.astype(BF16).reshape(SLICE, groups, ch)

    def activate(row, count):
        size = count * groups
        lhs = [big_g[pl.ds(row + a, count)].reshape(size, 2 * ch) for a in range(3)]
        out = dot(jnp.concatenate(lhs, axis=1), wc[...])
        for q in range(2):
            ct[pl.ds(q, size, stride=2), :] = out[:, q * ch : (q + 1) * ch]
        v = silu(ct[: 2 * size] + acc[pl.ds(row, count)].reshape(2 * size, ch))
        put_shifted(ys, v, row, count)

    def finish(row, count):
        pairs, rows = count // 2, pl.ds(row, count)
        skip = row % packs if isinstance(row, int) else packs - 2
        out = split_pairs(conv_pairs(ys, ws, row, count), count)
        packed = (skip + count + packs - 1) // packs
        if isinstance(row, int):
            at = (row - skip) // packs * width
        else:
            at = pl.multiple_of(lax.div(row - skip, packs) * width, width)
        lift = dot(mixed[pl.ds(at, packed * width)], wx[...])
        lifted = [
            lift[i // packs * width : (i // packs + 1) * width, i % packs * ch : (i % packs + 1) * ch]
            for i in range(skip, skip + count)
        ]
        own = f_ref[rows].reshape(pairs, 2, width, ch)
        results = []
        for q in range(2):
            pre = out[q] + jnp.stack(lifted[q::2])
            results.append((own[:, q].astype(F32) + silu(pre)).astype(BF16))
        o_ref[rows] = jnp.stack(results, axis=1).reshape(count, width, ch)

    project()
    send_projection()
    shift_features()
    clear_edges()
    for half in range(HALVES):
        fetch_context(half).wait()
    fetch(6).wait()
    fetch(7).wait()

    def pack_first():
        fetch(2).wait()
        pack_weights(wf, w1_ref)
        pack_context_weights()

    def pack_rest():
        for i in (3, 4, 5):
            fetch(i).wait()
        pack_weights(ws, w2_ref)
        pack_lead_weights()

    def wait_piece(copy, landed, c):
        for half in range(HALVES):
            copy(landed.at[c, half], c, half).wait_recv()

    edge = first | last

    @pl.when(edge)
    def _():
        pack_first()

        @pl.loop(0, chunks)
        def _(k):
            feature_conv(k)

        pack_rest()
        mix()

        def receive(c):
            @pl.when(first)
            def _():
                wait_piece(down_copy, down_in, c)

            @pl.when(last)
            def _():
                wait_piece(up_copy, up_in, c)

            take_context(c)

        @pl.loop(0, slices)
        def _(c):
            receive(c)

            @pl.when(c == 1)
            def _():
                activate(0, ROWS - 1)
                finish(0, ROWS - 2)

            @pl.when((c > 1) & (c < slices - 2) & (lax.rem(c, 2) == 1))
            def _():
                row = lax.div(c, 2) * ROWS
                activate(row - 1, ROWS)
                finish(row - 2, ROWS)

            @pl.when(c == slices - 2)
            def _():
                activate(height - ROWS - 1, SLICE)
                finish(height - ROWS - 2, SLICE)

    @pl.when(jnp.logical_not(edge))
    def _():
        up_at, down_at = LAG * z, LAG * (n - 1 - z)
        ready_at = jnp.maximum(up_at, down_at)
        up_first = up_at >= down_at
        start_at = jnp.minimum(up_at, down_at)
        owner = owner_ref[lead]
        mine = owner == z

        def go(at, copy, landed, out):
            c, half = lax.div(at, HALVES), lax.rem(at, HALVES)

            @pl.when((at >= 0) & (at < pieces))
            def _():
                copy(landed.at[c, half], c, half).wait_recv()
                out[c, half] = jnp.where(mine, c_ref[c, half], landed[c, half])
                copy(out.at[c, half], c, half).start()

        @pl.loop(start_at, ready_at + pieces)
        def _(s):
            @pl.when(up_first)
            def _():
                go(s - up_at, up_copy, up_in, up_out)
                go(s - down_at, down_copy, down_in, down_out)

            @pl.when(jnp.logical_not(up_first))
            def _():
                go(s - down_at, down_copy, down_in, down_out)
                go(s - up_at, up_copy, up_in, up_out)

            t = s - start_at

            @pl.when(t <= chunks + 2)
            def _():
                @pl.when(t == 0)
                def _():
                    pack_first()

                @pl.when((t >= 1) & (t <= chunks))
                def _():
                    feature_conv(t - 1)

                @pl.when(t == chunks + 1)
                def _():
                    pack_rest()

                @pl.when(t == chunks + 2)
                def _():
                    mix()

            r = s - ready_at

            @pl.when(r >= 1)
            def _():
                @pl.when(lax.rem(r, 2) == 1)
                def _():
                    take_context(lax.div(r, 2))

                @pl.when(r == ACT)
                def _():
                    activate(0, ROWS - 1)

                @pl.when(r == FIN)
                def _():
                    finish(0, ROWS - 2)

                ra = r - ACT

                @pl.when((ra >= 4) & (ra < 4 * (chunks - 1)) & (lax.rem(ra, 4) == 0))
                def _():
                    activate(ra * (ROWS // 4) - 1, ROWS)

                rf = r - FIN

                @pl.when((rf >= 4) & (rf < 4 * (chunks - 1)) & (lax.rem(rf, 4) == 0))
                def _():
                    finish(rf * (ROWS // 4) - 2, ROWS)

        activate(height - ROWS - 1, SLICE)
        finish(height - ROWS - 2, SLICE)

    activate(height - SLICE - 1, SLICE + 1)
    finish(height - SLICE - 2, SLICE + 2)

    @pl.loop(0, slices)
    def _(c):
        for half in range(HALVES):
            @pl.when(jnp.logical_not(last))
            def _():
                up_copy(c_ref.at[c, half], c, half).wait_send()

            @pl.when(jnp.logical_not(first))
            def _():
                down_copy(c_ref.at[c, half], c, half).wait_send()

    @pl.when(jnp.logical_not(lead_last))
    def _():
        lead_copy(0).wait_send()

    @pl.when(jnp.logical_not(lead_first))
    def _():
        lead_copy(1).wait_send()


def per_device(
    features, context, owner, hours, w_first, w_second, w_lead_in, w_lead_mix, w_lead_out
):
    n, leads = lax.axis_size("patch"), lax.axis_size("lead")
    _, _, height, width, ch = features.shape
    temporal = w_lead_in.shape[1]
    merged = context.shape[3]
    cells = ROWS * width
    groups = merged // ch
    packs = ch // temporal
    packed_rows = height * width // packs
    vmem = pltpu.VMEM
    slices = height // SLICE
    pieces = HALVES * slices
    line = vmem((slices, HALVES, SLICE, merged // HALVES), BF16)
    hbm = pl.BlockSpec(memory_space=pl.ANY)
    dma = pltpu.SemaphoreType.DMA
    out = pl.pallas_call(
        functools.partial(kernel, n, leads),
        out_shape=vmem((height, width, ch), BF16),
        in_specs=[hbm] * 9,
        out_specs=pl.BlockSpec(memory_space=pltpu.VMEM),
        scratch_shapes=[
            vmem((height, width, ch), BF16),
            line,
            vmem(w_first.shape, BF16),
            vmem(w_second.shape, BF16),
            vmem((temporal, ch), BF16),
            vmem(w_lead_mix.shape, BF16),
            vmem(w_lead_out.shape, BF16),
            vmem((3, height + 2, width, ch), BF16),
            vmem((3, height + 2, width, ch), BF16),
            vmem((height, width, ch), F32),
            vmem((height + 2, groups, 2 * ch), BF16),
            vmem((SLICE * groups, ch), F32),
            vmem((cells, ch), F32),
            vmem((12 * ch, 2 * ch), BF16),
            vmem((6 * ch, 2 * ch), BF16),
            vmem((12 * ch, 2 * ch), BF16),
            vmem((3, ch, ch), BF16),
            vmem((ch, packs * ch), BF16),
            vmem((ch, packs * ch), BF16),
            vmem((packed_rows, ch), BF16),
            vmem((packed_rows, ch), BF16),
            vmem((packed_rows, ch), BF16),
            vmem((packed_rows, ch), BF16),
            line, line, line, line,
            pltpu.SMEM(owner.shape, jnp.int32), pltpu.SMEM(hours.shape, jnp.int32),
            dma((HALVES,)), dma((8,)),
            dma((pieces,)), dma((pieces,)), dma((pieces,)), dma((pieces,)), dma((2,)), dma((2,)),
        ],
        compiler_params=pltpu.CompilerParams(collective_id=0, has_side_effects=True),
    )(
        owner, hours, features[0, 0], context.reshape(slices, SLICE, merged),
        w_first, w_second, w_lead_in.T, w_lead_mix, w_lead_out,
    )
    return out[None, None]


def solution(mesh):
    placed = (
        P(("grp", "lead"), "patch", None, None, None),
        P("patch", ("grp", "lead"), None, None),
        P("grp"),
        P("grp"),
        P(),
        P(),
        P(),
        P(),
        P(),
    )
    return jax.shard_map(
        per_device,
        mesh=mesh,
        in_specs=placed,
        out_specs=P(("grp", "lead"), "patch", None, None, None),
        check_vma=False,
    )
```

time: 28.7 us -> 27.6 us (0.962)
  Pallas kernels: 27.6 us -> 26.4 us
    pallas_call x1, Pallas kernels: 27.6 us -> 26.4 us  [per_device(): pl.pallas_call(functools.partial(kernel, n, leads), out_shape=vmem((heigh...]
where the time goes in v1:
time: 27.6 us; the launch traced here: 27.4 us
  Pallas kernels  26.4 us (96%)
  local copies, waits for them, and re-layouts  0.97 us (4%)
    pallas_call x1, Pallas kernels, per_device(): pl.pallas_call(functools.partial(kernel, n, leads), out_shape=vmem((heigh...  26.4 us
    unnamed x1, local copies, waits for them, and re-layouts  0.97 us

profile of v1, /device:TPU:0, one launch (start us, length us, event | category | flops | bytes accessed | tf_op | source)
XLA Modules:
  0.0 27.4 jit_solution(5658062588473827696)
XLA Ops:
  0.0 26.4 %shard_map.91 = bf16[128,32,128]{2,1,0:T(8,128)(2,1)S(1)} custom-call(s32[4]{0:T(128)} %owner_hbm.1, s32[4]{0:T(128)} %hours_hbm.1, bf16[128,32,128]{2,1,0:T(8,128)(2,1)} %bitcast.5, bf16[16,8,2048]{2,1,0:T(8,128)(2,1)} %bitcast.6, bf16[9,192,128]{2,1,0:T(8,128)(2,1)} %w1_hbm.1, bf16[9,128,128]{2,1,0:T(8,128)(2,1)} %w2_hbm.1, bf16[32,128]{1,0:T(8,128)(2,1)} %bitcast.7, ...), custom_call_target="tpu_custom_call" | custom-call | tf_op jit(solution)/shard_map/pallas_call | solution.py:501
  26.4 1.0 %copy.11 = bf16[1,1,128,32,128]{4,3,2,1,0:T(8,128)(2,1)} copy(bf16[1,1,128,32,128]{4,3,2,1,0:T(8,128)(2,1)S(1)} %bitcast.4) | data formatting | bytes 2097152

commit v2 on v1

--- a/solution.py
+++ b/solution.py
@@ -10,10 +10,9 @@
 MESH = pl.DeviceIdType.MESH
 ROWS = 16
 SLICE = 8
-HALVES = 2
-LAG = 9
-ACT = 3
-FIN = 5
+HALVES = 1
+LAG = 5
+EARLY = 2
 F32 = jnp.float32
 BF16 = jnp.bfloat16
 
@@ -313,15 +312,18 @@
     send_projection()
     shift_features()
     clear_edges()
+    fetch(2).wait()
+    pack_weights(wf, w1_ref)
+    pack_context_weights()
+
+    @pl.loop(0, EARLY)
+    def _(k):
+        feature_conv(k)
+
     for half in range(HALVES):
         fetch_context(half).wait()
     fetch(6).wait()
     fetch(7).wait()
-
-    def pack_first():
-        fetch(2).wait()
-        pack_weights(wf, w1_ref)
-        pack_context_weights()
 
     def pack_rest():
         for i in (3, 4, 5):
@@ -337,9 +339,7 @@
 
     @pl.when(edge)
     def _():
-        pack_first()
-
-        @pl.loop(0, chunks)
+        @pl.loop(EARLY, chunks)
         def _(k):
             feature_conv(k)
 
@@ -409,51 +409,44 @@
 
             t = s - start_at
 
-            @pl.when(t <= chunks + 2)
-            def _():
-                @pl.when(t == 0)
-                def _():
-                    pack_first()
-
-                @pl.when((t >= 1) & (t <= chunks))
-                def _():
-                    feature_conv(t - 1)
-
-                @pl.when(t == chunks + 1)
+            @pl.when(t <= chunks - EARLY + 1)
+            def _():
+                @pl.when(t < chunks - EARLY)
+                def _():
+                    feature_conv(t + EARLY)
+
+                @pl.when(t == chunks - EARLY)
                 def _():
                     pack_rest()
 
-                @pl.when(t == chunks + 2)
+                @pl.when(t == chunks - EARLY + 1)
                 def _():
                     mix()
 
             r = s - ready_at
 
-            @pl.when(r >= 1)
-            def _():
-                @pl.when(lax.rem(r, 2) == 1)
-                def _():
-                    take_context(lax.div(r, 2))
-
-                @pl.when(r == ACT)
+            @pl.when(r >= 0)
+            def _():
+                take_context(r)
+
+                @pl.when(r == 1)
                 def _():
                     activate(0, ROWS - 1)
 
-                @pl.when(r == FIN)
+                @pl.when(r == 2)
                 def _():
                     finish(0, ROWS - 2)
 
-                ra = r - ACT
-
-                @pl.when((ra >= 4) & (ra < 4 * (chunks - 1)) & (lax.rem(ra, 4) == 0))
-                def _():
-                    activate(ra * (ROWS // 4) - 1, ROWS)
-
-                rf = r - FIN
-
-                @pl.when((rf >= 4) & (rf < 4 * (chunks - 1)) & (lax.rem(rf, 4) == 0))
-                def _():
-                    finish(rf * (ROWS // 4) - 2, ROWS)
+                odd = lax.rem(r, 2)
+                row = (r - odd) * SLICE
+
+                @pl.when((r > 2) & (r < slices - 2) & (odd == 1))
+                def _():
+                    activate(row - 1, ROWS)
+
+                @pl.when((r > 2) & (odd == 0))
+                def _():
+                    finish(row - ROWS - 2, ROWS)
 
         activate(height - ROWS - 1, SLICE)
         finish(height - ROWS - 2, SLICE)

time: 27.6 us -> 26.9 us (0.975)
  Pallas kernels: 26.4 us -> 25.8 us
    pallas_call x1, Pallas kernels: 26.4 us -> 25.8 us  [per_device(): pl.pallas_call(functools.partial(kernel, n, leads), out_shape=vmem((heigh...]
where the time goes in v2:
time: 26.9 us; the launch traced here: 26.8 us
  Pallas kernels  25.8 us (96%)
  local copies, waits for them, and re-layouts  0.97 us (4%)
    pallas_call x1, Pallas kernels, per_device(): pl.pallas_call(functools.partial(kernel, n, leads), out_shape=vmem((heigh...  25.8 us
    unnamed x1, local copies, waits for them, and re-layouts  0.97 us

profile of v2, /device:TPU:0, one launch (start us, length us, event | category | flops | bytes accessed | tf_op | source)
XLA Modules:
  0.0 26.8 jit_solution(11205096921849188371)
XLA Ops:
  0.0 25.8 %shard_map.91 = bf16[128,32,128]{2,1,0:T(8,128)(2,1)S(1)} custom-call(s32[4]{0:T(128)} %owner_hbm.1, s32[4]{0:T(128)} %hours_hbm.1, bf16[128,32,128]{2,1,0:T(8,128)(2,1)} %bitcast.5, bf16[16,8,2048]{2,1,0:T(8,128)(2,1)} %bitcast.6, bf16[9,192,128]{2,1,0:T(8,128)(2,1)} %w1_hbm.1, bf16[9,128,128]{2,1,0:T(8,128)(2,1)} %w2_hbm.1, bf16[32,128]{1,0:T(8,128)(2,1)} %bitcast.7, ...), custom_call_target="tpu_custom_call" | custom-call | tf_op jit(solution)/shard_map/pallas_call | solution.py:494
  25.8 1.0 %copy.11 = bf16[1,1,128,32,128]{4,3,2,1,0:T(8,128)(2,1)} copy(bf16[1,1,128,32,128]{4,3,2,1,0:T(8,128)(2,1)S(1)} %bitcast.4) | data formatting | bytes 2097152

commit v3 on v2

--- a/solution.py
+++ b/solution.py
@@ -12,6 +12,7 @@
 SLICE = 8
 HALVES = 1
 LAG = 5
+LATE = 5
 EARLY = 2
 F32 = jnp.float32
 BF16 = jnp.bfloat16
@@ -28,7 +29,7 @@
 def kernel(
     n, leads, owner_hbm, hours_hbm, f_hbm, c_hbm, w1_hbm, w2_hbm, wi_hbm, wm_hbm, wo_hbm, o_ref,
     f_ref, c_ref, w1_ref, w2_ref, wi_ref, wm_ref, wo_ref,
-    xs, ys, acc, big_g, gt, ct, wf, wc, ws, wd, wp, wx, proj, prev, foll, mixed,
+    xs, ys, acc, big_g, gt, wf, wc, ws, wd, wp, proj, prev, foll, mixed,
     up_in, down_in, up_out, down_out, owner_ref, hours_ref, small_sem, in_sem,
     up_send, up_recv, down_send, down_recv, lead_send, lead_recv,
 ):
@@ -158,12 +159,13 @@
 
     def pack_lead_weights():
         wd[...] = jnp.zeros_like(wd)
-        wx[...] = jnp.zeros_like(wx)
+        ws[12 * ch :] = jnp.zeros((packs // 2 * ch, 2 * ch), BF16)
         for q in range(packs):
             at = slice(q * temporal, (q + 1) * temporal)
             for t in range(3):
                 wd[t, at, at] = wm_ref[t]
-            wx[at, q * ch : (q + 1) * ch] = wo_ref[...]
+            low = (12 + q // 2) * ch + q * temporal
+            ws[low : low + temporal, q % 2 * ch : (q % 2 + 1) * ch] = wo_ref[...]
 
     def put_shifted(target, v, row, count):
         size = count * width
@@ -203,7 +205,7 @@
         def _():
             lead_copy(1).start()
 
-    def conv_pairs(source, weights, row, count):
+    def conv_pairs(source, weights, row, count, more=()):
         pairs = count // 2
         parts = [
             source[b, pl.ds(row, count + 2)].reshape(pairs + 1, 2, width, ch) for b in range(3)
@@ -213,7 +215,7 @@
             for r in range(4)
             for b in range(3)
         ]
-        return dot(jnp.concatenate(lhs, axis=1), weights[...])
+        return dot(jnp.concatenate(lhs + list(more), axis=1), weights[...])
 
     def split_pairs(out, count):
         return [
@@ -282,30 +284,33 @@
         size = count * groups
         lhs = [big_g[pl.ds(row + a, count)].reshape(size, 2 * ch) for a in range(3)]
         out = dot(jnp.concatenate(lhs, axis=1), wc[...])
-        for q in range(2):
-            ct[pl.ds(q, size, stride=2), :] = out[:, q * ch : (q + 1) * ch]
-        v = silu(ct[: 2 * size] + acc[pl.ds(row, count)].reshape(2 * size, ch))
+        v = silu(out.reshape(2 * size, ch) + acc[pl.ds(row, count)].reshape(2 * size, ch))
         put_shifted(ys, v, row, count)
 
     def finish(row, count):
         pairs, rows = count // 2, pl.ds(row, count)
         skip = row % packs if isinstance(row, int) else packs - 2
-        out = split_pairs(conv_pairs(ys, ws, row, count), count)
+        skip = row % packs if isinstance(row, int) else packs - 2
         packed = (skip + count + packs - 1) // packs
         if isinstance(row, int):
             at = (row - skip) // packs * width
         else:
             at = pl.multiple_of(lax.div(row - skip, packs) * width, width)
-        lift = dot(mixed[pl.ds(at, packed * width)], wx[...])
-        lifted = [
-            lift[i // packs * width : (i // packs + 1) * width, i % packs * ch : (i % packs + 1) * ch]
-            for i in range(skip, skip + count)
-        ]
+        near = mixed[pl.ds(at, packed * width)]
+        none = jnp.zeros((width, ch), BF16)
+        more = []
+        for turn in range(packs // 2):
+            blocks = []
+            for i in range(skip, skip + count, 2):
+                m = i // packs
+                hit = i % packs // 2 == turn
+                blocks.append(near[m * width : (m + 1) * width] if hit else none)
+            more.append(jnp.concatenate(blocks, axis=0))
+        out = split_pairs(conv_pairs(ys, ws, row, count, more), count)
         own = f_ref[rows].reshape(pairs, 2, width, ch)
         results = []
         for q in range(2):
-            pre = out[q] + jnp.stack(lifted[q::2])
-            results.append((own[:, q].astype(F32) + silu(pre)).astype(BF16))
+            results.append((own[:, q].astype(F32) + silu(out[q])).astype(BF16))
         o_ref[rows] = jnp.stack(results, axis=1).reshape(count, width, ch)
 
     project()
@@ -372,10 +377,6 @@
                 activate(row - 1, ROWS)
                 finish(row - 2, ROWS)
 
-            @pl.when(c == slices - 2)
-            def _():
-                activate(height - ROWS - 1, SLICE)
-                finish(height - ROWS - 2, SLICE)
 
     @pl.when(jnp.logical_not(edge))
     def _():
@@ -395,7 +396,7 @@
                 out[c, half] = jnp.where(mine, c_ref[c, half], landed[c, half])
                 copy(out.at[c, half], c, half).start()
 
-        @pl.loop(start_at, ready_at + pieces)
+        @pl.loop(start_at, ready_at + pieces + LATE)
         def _(s):
             @pl.when(up_first)
             def _():
@@ -423,7 +424,7 @@
                 def _():
                     mix()
 
-            r = s - ready_at
+            r = s - ready_at - LATE
 
             @pl.when(r >= 0)
             def _():
@@ -448,11 +449,8 @@
                 def _():
                     finish(row - ROWS - 2, ROWS)
 
-        activate(height - ROWS - 1, SLICE)
-        finish(height - ROWS - 2, SLICE)
-
-    activate(height - SLICE - 1, SLICE + 1)
-    finish(height - SLICE - 2, SLICE + 2)
+    activate(height - ROWS - 1, ROWS + 1)
+    finish(height - ROWS - 2, ROWS + 2)
 
     @pl.loop(0, slices)
     def _(c):
@@ -509,12 +507,10 @@
             vmem((height, width, ch), F32),
             vmem((height + 2, groups, 2 * ch), BF16),
             vmem((SLICE * groups, ch), F32),
-            vmem((cells, ch), F32),
             vmem((12 * ch, 2 * ch), BF16),
             vmem((6 * ch, 2 * ch), BF16),
-            vmem((12 * ch, 2 * ch), BF16),
+            vmem(((12 + packs // 2) * ch, 2 * ch), BF16),
             vmem((3, ch, ch), BF16),
-            vmem((ch, packs * ch), BF16),
             vmem((ch, packs * ch), BF16),
             vmem((packed_rows, ch), BF16),
             vmem((packed_rows, ch), BF16),

time: 26.9 us -> 26.3 us (0.978)
  Pallas kernels: 25.8 us -> 25.2 us
    pallas_call x1, Pallas kernels: 25.8 us -> 25.2 us  [per_device(): pl.pallas_call(functools.partial(kernel, n, leads), out_shape=vmem((heigh...]
where the time goes in v3:
time: 26.3 us; the launch traced here: 26.1 us
  Pallas kernels  25.2 us (96%)
  local copies, waits for them, and re-layouts  0.97 us (4%)
    pallas_call x1, Pallas kernels, per_device(): pl.pallas_call(functools.partial(kernel, n, leads), out_shape=vmem((heigh...  25.2 us
    unnamed x1, local copies, waits for them, and re-layouts  0.97 us

profile of v3, /device:TPU:0, one launch (start us, length us, event | category | flops | bytes accessed | tf_op | source)
XLA Modules:
  0.0 26.1 jit_solution(1726385181615494145)
XLA Ops:
  0.0 25.2 %shard_map.91 = bf16[128,32,128]{2,1,0:T(8,128)(2,1)S(1)} custom-call(s32[4]{0:T(128)} %owner_hbm.1, s32[4]{0:T(128)} %hours_hbm.1, bf16[128,32,128]{2,1,0:T(8,128)(2,1)} %bitcast.5, bf16[16,8,2048]{2,1,0:T(8,128)(2,1)} %bitcast.6, bf16[9,192,128]{2,1,0:T(8,128)(2,1)} %w1_hbm.1, bf16[9,128,128]{2,1,0:T(8,128)(2,1)} %w2_hbm.1, bf16[32,128]{1,0:T(8,128)(2,1)} %bitcast.7, ...), custom_call_target="tpu_custom_call" | custom-call | tf_op jit(solution)/shard_map/pallas_call | solution.py:492
  25.2 1.0 %copy.11 = bf16[1,1,128,32,128]{4,3,2,1,0:T(8,128)(2,1)} copy(bf16[1,1,128,32,128]{4,3,2,1,0:T(8,128)(2,1)S(1)} %bitcast.4) | data formatting | bytes 2097152

commit v4 on v3

--- a/solution.py
+++ b/solution.py
@@ -12,6 +12,7 @@
 SLICE = 8
 HALVES = 1
 LAG = 5
+LIMIT = 56 * 2**20
 LATE = 5
 EARLY = 2
 F32 = jnp.float32
@@ -26,10 +27,71 @@
     return jnp.dot(a, b, preferred_element_type=F32)
 
 
+def conv_pairs(source, weights, row, count, more=()):
+    width, ch = source.shape[2:]
+    pairs = count // 2
+    parts = [
+        source[b, pl.ds(row, count + 2)].reshape(pairs + 1, 2, width, ch) for b in range(3)
+    ]
+    lhs = [
+        parts[b][r // 2 : r // 2 + pairs, r % 2].reshape(pairs * width, ch)
+        for r in range(4)
+        for b in range(3)
+    ]
+    return dot(jnp.concatenate(lhs + list(more), axis=1), weights[...])
+
+def split_pairs(out, count, width):
+    ch = out.shape[1] // 2
+    return [
+        out[:, q * ch : (q + 1) * ch].reshape(count // 2, width, ch) for q in range(2)
+    ]
+
+
+def finished(f_ref, ys, ws, mixed, row, count):
+    height, width, ch = f_ref.shape
+    packs = height * width // mixed.shape[0]
+    pairs, rows = count // 2, pl.ds(row, count)
+    skip = row % packs if isinstance(row, int) else packs - 2
+    skip = row % packs if isinstance(row, int) else packs - 2
+    packed = (skip + count + packs - 1) // packs
+    if isinstance(row, int):
+        at = (row - skip) // packs * width
+    else:
+        at = pl.multiple_of(lax.div(row - skip, packs) * width, width)
+    near = mixed[pl.ds(at, packed * width)]
+    none = jnp.zeros((width, ch), BF16)
+    more = []
+    for turn in range(packs // 2):
+        blocks = []
+        for i in range(skip, skip + count, 2):
+            m = i // packs
+            hit = i % packs // 2 == turn
+            blocks.append(near[m * width : (m + 1) * width] if hit else none)
+        more.append(jnp.concatenate(blocks, axis=0))
+    out = split_pairs(conv_pairs(ys, ws, row, count, more), count, width)
+    own = f_ref[rows].reshape(pairs, 2, width, ch)
+    results = []
+    for q in range(2):
+        results.append((own[:, q].astype(F32) + silu(out[q])).astype(BF16))
+    return jnp.stack(results, axis=1).reshape(count, width, ch)
+
+
+def last_rows(o_in, f_ref, ys, ws, mixed, out_hbm, rest, sem):
+    height = f_ref.shape[0]
+    start = height - ROWS - 2
+    early = pltpu.make_async_copy(o_in.at[:start], out_hbm.at[:start], sem.at[0])
+    early.start()
+    rest[...] = finished(f_ref, ys, ws, mixed, start, ROWS + 2)
+    late = pltpu.make_async_copy(rest, out_hbm.at[start:], sem.at[1])
+    late.start()
+    early.wait()
+    late.wait()
+
+
 def kernel(
-    n, leads, owner_hbm, hours_hbm, f_hbm, c_hbm, w1_hbm, w2_hbm, wi_hbm, wm_hbm, wo_hbm, o_ref,
-    f_ref, c_ref, w1_ref, w2_ref, wi_ref, wm_ref, wo_ref,
-    xs, ys, acc, big_g, gt, wf, wc, ws, wd, wp, proj, prev, foll, mixed,
+    n, leads, owner_hbm, hours_hbm, f_hbm, c_hbm, w1_hbm, w2_hbm, wi_hbm, wm_hbm, wo_hbm, o_ref, f_ref, ys, ws, mixed,
+    c_ref, w1_ref, w2_ref, wi_ref, wm_ref, wo_ref,
+    xs, acc, big_g, gt, wf, wc, wd, wp, proj, prev, foll,
     up_in, down_in, up_out, down_out, owner_ref, hours_ref, small_sem, in_sem,
     up_send, up_recv, down_send, down_recv, lead_send, lead_recv,
 ):
@@ -205,25 +267,8 @@
         def _():
             lead_copy(1).start()
 
-    def conv_pairs(source, weights, row, count, more=()):
-        pairs = count // 2
-        parts = [
-            source[b, pl.ds(row, count + 2)].reshape(pairs + 1, 2, width, ch) for b in range(3)
-        ]
-        lhs = [
-            parts[b][r // 2 : r // 2 + pairs, r % 2].reshape(pairs * width, ch)
-            for r in range(4)
-            for b in range(3)
-        ]
-        return dot(jnp.concatenate(lhs + list(more), axis=1), weights[...])
-
-    def split_pairs(out, count):
-        return [
-            out[:, q * ch : (q + 1) * ch].reshape(count // 2, width, ch) for q in range(2)
-        ]
-
     def feature_conv(k):
-        out = split_pairs(conv_pairs(xs, wf, k * ROWS, ROWS), ROWS)
+        out = split_pairs(conv_pairs(xs, wf, k * ROWS, ROWS), ROWS, width)
         acc[pl.ds(k * ROWS, ROWS)] = jnp.stack(out, axis=1).reshape(ROWS, width, ch)
 
     def mix():
@@ -288,30 +333,7 @@
         put_shifted(ys, v, row, count)
 
     def finish(row, count):
-        pairs, rows = count // 2, pl.ds(row, count)
-        skip = row % packs if isinstance(row, int) else packs - 2
-        skip = row % packs if isinstance(row, int) else packs - 2
-        packed = (skip + count + packs - 1) // packs
-        if isinstance(row, int):
-            at = (row - skip) // packs * width
-        else:
-            at = pl.multiple_of(lax.div(row - skip, packs) * width, width)
-        near = mixed[pl.ds(at, packed * width)]
-        none = jnp.zeros((width, ch), BF16)
-        more = []
-        for turn in range(packs // 2):
-            blocks = []
-            for i in range(skip, skip + count, 2):
-                m = i // packs
-                hit = i % packs // 2 == turn
-                blocks.append(near[m * width : (m + 1) * width] if hit else none)
-            more.append(jnp.concatenate(blocks, axis=0))
-        out = split_pairs(conv_pairs(ys, ws, row, count, more), count)
-        own = f_ref[rows].reshape(pairs, 2, width, ch)
-        results = []
-        for q in range(2):
-            results.append((own[:, q].astype(F32) + silu(out[q])).astype(BF16))
-        o_ref[rows] = jnp.stack(results, axis=1).reshape(count, width, ch)
+        o_ref[pl.ds(row, count)] = finished(f_ref, ys, ws, mixed, row, count)
 
     project()
     send_projection()
@@ -450,7 +472,6 @@
                     finish(row - ROWS - 2, ROWS)
 
     activate(height - ROWS - 1, ROWS + 1)
-    finish(height - ROWS - 2, ROWS + 2)
 
     @pl.loop(0, slices)
     def _(c):
@@ -489,13 +510,19 @@
     line = vmem((slices, HALVES, SLICE, merged // HALVES), BF16)
     hbm = pl.BlockSpec(memory_space=pl.ANY)
     dma = pltpu.SemaphoreType.DMA
-    out = pl.pallas_call(
+    held = [
+        vmem((height, width, ch), BF16),
+        vmem((height, width, ch), BF16),
+        vmem((3, height + 2, width, ch), BF16),
+        vmem(((12 + packs // 2) * ch, 2 * ch), BF16),
+        vmem((packed_rows, ch), BF16),
+    ]
+    most = pl.pallas_call(
         functools.partial(kernel, n, leads),
-        out_shape=vmem((height, width, ch), BF16),
+        out_shape=held,
         in_specs=[hbm] * 9,
-        out_specs=pl.BlockSpec(memory_space=pltpu.VMEM),
+        out_specs=[pl.BlockSpec(memory_space=pltpu.VMEM)] * len(held),
         scratch_shapes=[
-            vmem((height, width, ch), BF16),
             line,
             vmem(w_first.shape, BF16),
             vmem(w_second.shape, BF16),
@@ -503,16 +530,13 @@
             vmem(w_lead_mix.shape, BF16),
             vmem(w_lead_out.shape, BF16),
             vmem((3, height + 2, width, ch), BF16),
-            vmem((3, height + 2, width, ch), BF16),
             vmem((height, width, ch), F32),
             vmem((height + 2, groups, 2 * ch), BF16),
             vmem((SLICE * groups, ch), F32),
             vmem((12 * ch, 2 * ch), BF16),
             vmem((6 * ch, 2 * ch), BF16),
-            vmem(((12 + packs // 2) * ch, 2 * ch), BF16),
             vmem((3, ch, ch), BF16),
             vmem((ch, packs * ch), BF16),
-            vmem((packed_rows, ch), BF16),
             vmem((packed_rows, ch), BF16),
             vmem((packed_rows, ch), BF16),
             vmem((packed_rows, ch), BF16),
@@ -521,11 +545,21 @@
             dma((HALVES,)), dma((8,)),
             dma((pieces,)), dma((pieces,)), dma((pieces,)), dma((pieces,)), dma((2,)), dma((2,)),
         ],
-        compiler_params=pltpu.CompilerParams(collective_id=0, has_side_effects=True),
+        compiler_params=pltpu.CompilerParams(
+            collective_id=0, has_side_effects=True, vmem_limit_bytes=LIMIT
+        ),
     )(
         owner, hours, features[0, 0], context.reshape(slices, SLICE, merged),
         w_first, w_second, w_lead_in.T, w_lead_mix, w_lead_out,
     )
+    out = pl.pallas_call(
+        last_rows,
+        out_shape=jax.ShapeDtypeStruct((height, width, ch), BF16),
+        in_specs=[pl.BlockSpec(memory_space=pltpu.VMEM)] * len(held),
+        out_specs=hbm,
+        scratch_shapes=[vmem((ROWS + 2, width, ch), BF16), dma((2,))],
+        compiler_params=pltpu.CompilerParams(vmem_limit_bytes=16 * 2**20),
+    )(*most)
     return out[None, None]
 
 

time: 26.3 us -> 25.9 us (0.985)
  local copies, waits for them, and re-layouts: 0.97 us -> 0 us
  Pallas kernels: 25.2 us -> 25.7 us
    unnamed x1 -> x0, local copies, waits for them, and re-layouts: 0.97 us -> none
    pallas_call x1 -> x2, Pallas kernels: 25.2 us -> 25.7 us  [the longest x1 24.6 us: per_device(): pl.pallas_call(functools.partial(kernel, n, leads), out_shape=held, in_sp...]
where the time goes in v4:
time: 25.9 us; the launch traced here: 25.7 us
  Pallas kernels  25.7 us (99%)
    pallas_call x1, Pallas kernels, per_device(): pl.pallas_call(functools.partial(kernel, n, leads), out_shape=held, in_sp...  24.6 us
    pallas_call x1, Pallas kernels, per_device(): pl.pallas_call(last_rows, out_shape=jax.ShapeDtypeStruct((height, width,...  1.13 us

profile of v4, /device:TPU:0, one launch (start us, length us, event | category | flops | bytes accessed | tf_op | source)
XLA Modules:
  0.0 25.7 jit_solution(2738975437587963340)
XLA Ops:
  0.0 24.6 %shard_map.91 = (bf16[128,32,128]{2,1,0:T(8,128)(2,1)S(1)}, bf16[128,32,128]{2,1,0:T(8,128)(2,1)S(1)}, bf16[3,130,32,128]{3,2,1,0:T(8,128)(2,1)S(1)}, bf16[1792,256]{1,0:T(8,128)(2,1)S(1)}, bf16[1024,128]{1,0:T(8,128)(2,1)S(1)}) custom-call(s32[4]{0:T(128)} %owner_hbm.1, s32[4]{0:T(128)} %hours_hbm.1, bf16[128,32,128]{2,1,0:T(8,128)(2,1)} %bitcast.4, ...), custom_call_target="tpu_custom_call" | custom-call | tf_op jit(solution)/shard_map/pallas_call | solution.py:520
  24.6 1.1 %shard_map.92 = bf16[128,32,128]{2,1,0:T(8,128)(2,1)} custom-call(bf16[128,32,128]{2,1,0:T(8,128)(2,1)S(1)} %get-tuple-element.10.o_in, bf16[128,32,128]{2,1,0:T(8,128)(2,1)S(1)} %get-tuple-element.11.f_ref, bf16[3,130,32,128]{3,2,1,0:T(8,128)(2,1)S(1)} %get-tuple-element.12.ys, bf16[1792,256]{1,0:T(8,128)(2,1)S(1)} %get-tuple-element.13.ws, ...), custom_call_target="tpu_custom_call" | custom-call | tf_op jit(solution)/shard_map/pallas_call | solution.py:555

commit v5 on v4

--- a/solution.py
+++ b/solution.py
@@ -14,7 +14,8 @@
 LAG = 5
 LIMIT = 56 * 2**20
 LATE = 5
-EARLY = 2
+PARTS = 4
+EARLY = 3
 F32 = jnp.float32
 BF16 = jnp.bfloat16
 
@@ -271,7 +272,7 @@
         out = split_pairs(conv_pairs(xs, wf, k * ROWS, ROWS), ROWS, width)
         acc[pl.ds(k * ROWS, ROWS)] = jnp.stack(out, axis=1).reshape(ROWS, width, ch)
 
-    def mix():
+    def mix_wait():
         @pl.when(jnp.logical_not(lead_first))
         def _():
             lead_copy(0).wait_recv()
@@ -288,6 +289,7 @@
         def _():
             foll[...] = jnp.zeros_like(foll)
 
+    def mix(i):
         now = hours_ref[lead]
         before = hours_ref[jnp.maximum(lead - 1, 0)]
         after = hours_ref[jnp.minimum(lead + 1, leads - 1)]
@@ -298,10 +300,12 @@
 
         gain_prev = gain(now, before, lead_first)
         gain_next = gain(after, now, lead_last)
-        value = gain_prev * dot(prev[...], wd[0])
-        value = value + dot(proj[...], wd[1])
-        value = value + gain_next * dot(foll[...], wd[2])
-        mixed[...] = value.astype(BF16)
+        size = packed_rows // PARTS
+        rows = pl.ds(pl.multiple_of(i * size, size), size)
+        value = gain_prev * dot(prev[rows], wd[0])
+        value = value + dot(proj[rows], wd[1])
+        value = value + gain_next * dot(foll[rows], wd[2])
+        mixed[rows] = value.astype(BF16)
 
     total_rows = SLICE * groups
 
@@ -371,7 +375,12 @@
             feature_conv(k)
 
         pack_rest()
-        mix()
+        mix_wait()
+
+        @pl.loop(0, PARTS)
+        def _(i):
+            mix(i)
+
 
         def receive(c):
             @pl.when(first)
@@ -432,7 +441,9 @@
 
             t = s - start_at
 
-            @pl.when(t <= chunks - EARLY + 1)
+            mix_at = chunks - EARLY + 1
+
+            @pl.when(t < mix_at + PARTS)
             def _():
                 @pl.when(t < chunks - EARLY)
                 def _():
@@ -442,9 +453,13 @@
                 def _():
                     pack_rest()
 
-                @pl.when(t == chunks - EARLY + 1)
-                def _():
-                    mix()
+                @pl.when(t == mix_at)
+                def _():
+                    mix_wait()
+
+                @pl.when(t >= mix_at)
+                def _():
+                    mix(t - mix_at)
 
             r = s - ready_at - LATE
 

time: 25.9 us -> 25.9 us (level)
  no operation moved by 1% of the time
where the time goes in v5:
time: 25.9 us; the launch traced here: 25.7 us
  Pallas kernels  25.7 us (99%)
    pallas_call x1, Pallas kernels, per_device(): pl.pallas_call(functools.partial(kernel, n, leads), out_shape=held, in_sp...  24.6 us
    pallas_call x1, Pallas kernels, per_device(): pl.pallas_call(last_rows, out_shape=jax.ShapeDtypeStruct((height, width,...  1.13 us

profile of v5, /device:TPU:0, one launch (start us, length us, event | category | flops | bytes accessed | tf_op | source)
XLA Modules:
  0.0 25.7 jit_solution(13344522528865297249)
XLA Ops:
  0.0 24.6 %shard_map.91 = (bf16[128,32,128]{2,1,0:T(8,128)(2,1)S(1)}, bf16[128,32,128]{2,1,0:T(8,128)(2,1)S(1)}, bf16[3,130,32,128]{3,2,1,0:T(8,128)(2,1)S(1)}, bf16[1792,256]{1,0:T(8,128)(2,1)S(1)}, bf16[1024,128]{1,0:T(8,128)(2,1)S(1)}) custom-call(s32[4]{0:T(128)} %owner_hbm.1, s32[4]{0:T(128)} %hours_hbm.1, bf16[128,32,128]{2,1,0:T(8,128)(2,1)} %bitcast.4, ...), custom_call_target="tpu_custom_call" | custom-call | tf_op jit(solution)/shard_map/pallas_call | solution.py:535
  24.6 1.1 %shard_map.92 = bf16[128,32,128]{2,1,0:T(8,128)(2,1)} custom-call(bf16[128,32,128]{2,1,0:T(8,128)(2,1)S(1)} %get-tuple-element.10.o_in, bf16[128,32,128]{2,1,0:T(8,128)(2,1)S(1)} %get-tuple-element.11.f_ref, bf16[3,130,32,128]{3,2,1,0:T(8,128)(2,1)S(1)} %get-tuple-element.12.ys, bf16[1792,256]{1,0:T(8,128)(2,1)S(1)} %get-tuple-element.13.ws, ...), custom_call_target="tpu_custom_call" | custom-call | tf_op jit(solution)/shard_map/pallas_call | solution.py:570

commit v6 on v5

--- a/solution.py
+++ b/solution.py
@@ -151,9 +151,6 @@
         fetch(i).start()
     for half in range(HALVES):
         fetch_context(half).start()
-    for i in range(2, 6):
-        fetch(i).start()
-
     pl.semaphore_wait(barrier, neighbours)
 
     def up_copy(src, c, half):
@@ -183,6 +180,9 @@
         def _(c):
             for half in range(HALVES):
                 down_copy(c_hbm.at[c, :, half * part : (half + 1) * part], c, half).start()
+
+    for i in range(2, 6):
+        fetch(i).start()
 
     def project():
         fetch(0).wait()

time: 25.9 us -> 25.9 us (level)
  no operation moved by 1% of the time
where the time goes in v6:
time: 25.9 us; the launch traced here: 25.7 us
  Pallas kernels  25.7 us (99%)
    pallas_call x1, Pallas kernels, per_device(): pl.pallas_call(functools.partial(kernel, n, leads), out_shape=held, in_sp...  24.6 us
    pallas_call x1, Pallas kernels, per_device(): pl.pallas_call(last_rows, out_shape=jax.ShapeDtypeStruct((height, width,...  1.13 us

profile of v6, /device:TPU:0, one launch (start us, length us, event | category | flops | bytes accessed | tf_op | source)
XLA Modules:
  0.0 25.7 jit_solution(8962214424409289994)
XLA Ops:
  0.0 24.6 %shard_map.91 = (bf16[128,32,128]{2,1,0:T(8,128)(2,1)S(1)}, bf16[128,32,128]{2,1,0:T(8,128)(2,1)S(1)}, bf16[3,130,32,128]{3,2,1,0:T(8,128)(2,1)S(1)}, bf16[1792,256]{1,0:T(8,128)(2,1)S(1)}, bf16[1024,128]{1,0:T(8,128)(2,1)S(1)}) custom-call(s32[4]{0:T(128)} %owner_hbm.1, s32[4]{0:T(128)} %hours_hbm.1, bf16[128,32,128]{2,1,0:T(8,128)(2,1)} %bitcast.4, ...), custom_call_target="tpu_custom_call" | custom-call | tf_op jit(solution)/shard_map/pallas_call | solution.py:535
  24.6 1.1 %shard_map.92 = bf16[128,32,128]{2,1,0:T(8,128)(2,1)} custom-call(bf16[128,32,128]{2,1,0:T(8,128)(2,1)S(1)} %get-tuple-element.10.o_in, bf16[128,32,128]{2,1,0:T(8,128)(2,1)S(1)} %get-tuple-element.11.f_ref, bf16[3,130,32,128]{3,2,1,0:T(8,128)(2,1)S(1)} %get-tuple-element.12.ys, bf16[1792,256]{1,0:T(8,128)(2,1)S(1)} %get-tuple-element.13.ws, ...), custom_call_target="tpu_custom_call" | custom-call | tf_op jit(solution)/shard_map/pallas_call | solution.py:570

commit v7 on v5

--- a/solution.py
+++ b/solution.py
@@ -13,7 +13,7 @@
 HALVES = 1
 LAG = 5
 LIMIT = 56 * 2**20
-LATE = 5
+LATE = 6
 PARTS = 4
 EARLY = 3
 F32 = jnp.float32

time: 25.9 us -> 25.9 us (level)
  no operation moved by 1% of the time
where the time goes in v7:
time: 25.9 us; the launch traced here: 25.7 us
  Pallas kernels  25.7 us (99%)
    pallas_call x1, Pallas kernels, per_device(): pl.pallas_call(functools.partial(kernel, n, leads), out_shape=held, in_sp...  24.6 us
    pallas_call x1, Pallas kernels, per_device(): pl.pallas_call(last_rows, out_shape=jax.ShapeDtypeStruct((height, width,...  1.13 us

profile of v7, /device:TPU:0, one launch (start us, length us, event | category | flops | bytes accessed | tf_op | source)
XLA Modules:
  0.0 25.7 jit_solution(9491686741681752237)
XLA Ops:
  0.0 24.6 %shard_map.91 = (bf16[128,32,128]{2,1,0:T(8,128)(2,1)S(1)}, bf16[128,32,128]{2,1,0:T(8,128)(2,1)S(1)}, bf16[3,130,32,128]{3,2,1,0:T(8,128)(2,1)S(1)}, bf16[1792,256]{1,0:T(8,128)(2,1)S(1)}, bf16[1024,128]{1,0:T(8,128)(2,1)S(1)}) custom-call(s32[4]{0:T(128)} %owner_hbm.1, s32[4]{0:T(128)} %hours_hbm.1, bf16[128,32,128]{2,1,0:T(8,128)(2,1)} %bitcast.4, ...), custom_call_target="tpu_custom_call" | custom-call | tf_op jit(solution)/shard_map/pallas_call | solution.py:535
  24.6 1.1 %shard_map.92 = bf16[128,32,128]{2,1,0:T(8,128)(2,1)} custom-call(bf16[128,32,128]{2,1,0:T(8,128)(2,1)S(1)} %get-tuple-element.10.o_in, bf16[128,32,128]{2,1,0:T(8,128)(2,1)S(1)} %get-tuple-element.11.f_ref, bf16[3,130,32,128]{3,2,1,0:T(8,128)(2,1)S(1)} %get-tuple-element.12.ys, bf16[1792,256]{1,0:T(8,128)(2,1)S(1)} %get-tuple-element.13.ws, ...), custom_call_target="tpu_custom_call" | custom-call | tf_op jit(solution)/shard_map/pallas_call | solution.py:570
